TPU v7x, 32 devices: a whole 2x2x4 slice. The times are simulated.
32 devices in a mesh: query: 8 (over z, y), store: 4 (over x, core).
Axes of the slice: x: 2, y: 2, z: 4, core: 2. Of those that a mesh axis runs over, the one named last changes fastest.
Arguments:
- in_rows: bfloat16 [8, 16384, 64], P('query', 'store'), may hold values from -6 to 6
- out_rows: bfloat16 [8, 16384, 128], P('query', 'store'), may hold values from -0.625 to 0.625
- row_doc: int32 [8, 16384], P('query', 'store'), may hold values from 0 to 31
- row_pos: int32 [8, 16384], P('query', 'store'), may hold values from 0 to 255
- doc_len: int32 [8, 128], P('query', 'store'), may hold values from 128 to 256
- eig_in: float32 [64], replicated, may hold values from 0.25 to 2
- eig_out: float32 [128], replicated, may hold values from 0.25 to 2
- basis_in: float32 [64, 64], replicated, may hold values from -0.75 to 0.75
- basis_out: float32 [128, 128], replicated, may hold values from -0.5 to 0.5
- train_feats: bfloat16 [8, 768, 8192], P('query', 'store'), may hold values from -0.0625 to 0.0625
Outputs:
- scores: bfloat16 [8, 128, 768], P('query', None, 'store')
Inputs may be any that keep to these rules, and one draw needn't show every extreme that they name: On each device the 4096 rows form 8 blocks of 512 rows in order; the rows of block j belong to documents of group j in the same store column, and row_doc names the document among that destination's 32.
All inputs are finite; a program needn't handle non-finite values.
Results may differ from a plain program's by a relative error of at most 0.0049.
Values may be sent and summed in bfloat16 or wider, within the bound.
A program may use at most 64 MiB of HBM per device.

v0:
```python
import math

import jax
import jax.numpy as jnp
from jax import lax
from jax.sharding import PartitionSpec as P

damping = 0.1
highest = lax.Precision.HIGHEST


def from_behind(x, axis, by):
    devices = lax.axis_size(axis)
    return lax.ppermute(x, axis, [(i, (i + by) % devices) for i in range(devices)])


def precondition(gradients, scaling, basis_in, basis_out):
    in_width = basis_in.shape[0]
    out_width = basis_out.shape[0]
    doc_count = gradients.shape[1] // in_width
    rotated = jnp.dot(basis_out.T, gradients, precision=highest)
    turned = jnp.dot(rotated.reshape(out_width * doc_count, in_width), basis_in, precision=highest)
    turned = turned.reshape(out_width, doc_count, in_width) * scaling[:, None, :]
    restored = jnp.dot(
        basis_out, turned.reshape(out_width, doc_count * in_width), precision=highest
    )
    final_map = jnp.dot(
        restored.reshape(out_width * doc_count, in_width), basis_in.T, precision=highest
    )
    final_map = final_map.reshape(out_width, doc_count, in_width)
    return (
        jnp.transpose(final_map, (1, 0, 2))
        .reshape(doc_count, out_width * in_width)
        .astype(jnp.bfloat16)
    )


def record(score_table, query_block, anchor, train_slab):
    partial_scores = lax.dot_general(
        query_block, train_slab, (((1,), (1,)), ((), ())), preferred_element_type=jnp.float32
    )
    return lax.dynamic_update_slice_in_dim(
        score_table, partial_scores.astype(jnp.bfloat16), anchor * query_block.shape[0], 0
    )


def on_device(
    in_rows, out_rows, row_doc, row_pos, doc_len, eig_in, eig_out, basis_in, basis_out, train_feats
):
    doc_count = doc_len.shape[1]
    in_width = in_rows.shape[2]
    packed_keys = row_doc * 65536 + row_pos
    inputs_side, grads_side, keys_side = (
        lax.all_to_all(in_rows, "query", split_axis=1, concat_axis=1, tiled=True),
        lax.all_to_all(out_rows, "query", split_axis=1, concat_axis=1, tiled=True),
        lax.all_to_all(packed_keys, "query", split_axis=1, concat_axis=1, tiled=True),
    )
    inputs_side = inputs_side[0]
    grads_side = grads_side[0]
    keys_side = keys_side[0]
    doc_of_row = keys_side // 65536
    pos_of_row = keys_side % 65536
    live_mask = (doc_of_row[:, None] == jnp.arange(doc_count, dtype=jnp.int32)[None, :]) & (
        pos_of_row[:, None] < doc_len[0][None, :]
    )
    weights = live_mask.astype(jnp.bfloat16)
    row_count = inputs_side.shape[0]
    row_span = math.gcd(row_count, 1024)

    def accumulate(turn_index, running):
        row_start = turn_index * row_span
        x_part = lax.dynamic_slice_in_dim(inputs_side, row_start, row_span, 0)
        g_part = lax.dynamic_slice_in_dim(grads_side, row_start, row_span, 0)
        w_part = lax.dynamic_slice_in_dim(weights, row_start, row_span, 0)
        spread = (w_part[:, :, None] * x_part[:, None, :]).reshape(row_span, doc_count * in_width)
        return running + lax.dot_general(
            g_part, spread, (((0,), (0,)), ((), ())), preferred_element_type=jnp.float32
        )

    gradients = jnp.zeros((grads_side.shape[1], doc_count * in_width), jnp.float32)
    gradients = lax.fori_loop(0, row_count // row_span, accumulate, gradients)
    scaling = 1.0 / (eig_out[:, None] * eig_in[None, :] + damping)
    query_block = precondition(gradients, scaling, basis_in, basis_out)
    train_slab = train_feats[0]
    store_count = lax.axis_size("store")
    own_index = lax.axis_index("store")
    score_table = jnp.zeros((store_count * doc_count, train_slab.shape[0]), jnp.bfloat16)

    def travel(carry, visit_index):
        moving, table_now = carry
        table_now = record(table_now, moving, (own_index - visit_index) % store_count, train_slab)
        moving = from_behind(moving, "store", 1)
        return ((moving, table_now), None)

    (moving, score_table), _ = lax.scan(
        travel, (query_block, score_table), jnp.arange(store_count - 1, dtype=jnp.int32)
    )
    score_table = record(
        score_table, moving, (own_index - (store_count - 1)) % store_count, train_slab
    )
    return score_table[None]


def solution(mesh):
    placed = (
        P("query", "store", None),
        P("query", "store", None),
        P("query", "store"),
        P("query", "store"),
        P("query", "store"),
        P(),
        P(),
        P(),
        P(),
        P("query", "store", None),
    )
    return jax.shard_map(
        on_device, mesh=mesh, in_specs=placed, out_specs=P("query", None, "store"), check_vma=False
    )
```

profile of v0, /device:TPU:0, one launch (start us, length us, event | category | flops | bytes accessed | tf_op | source)
XLA Modules:
  0.0 183.5 jit_solution(18066739965186172153)
XLA Ops:
  1.4 7.3 %all-to-all-start.1 = ((s32[1,8,512]{2,0,1:T(1,128)}), s32[1,8,512]{2,0,1:T(1,128)S(1)}, u32[]{:S(2)}, u32[]{:S(2)}) async-start(s32[1,8,512]{2,0,1:T(1,128)} %bitcast.1), calls=%async_computation.1 | async-start | bytes 32768 | tf_op jit(solution)/shard_map/all_to_all | solution.py:56
  8.7 4.9 %copy.27 = bf16[1,4096,64]{2,0,1:T(2,128)(2,1)S(1)} copy(bf16[1,4096,64]{1,2,0:T(8,128)(2,1)} %param.14) | data formatting | bytes 1048576 | tf_op args[0]
  14.1 22.3 %reduce.1 = bf16[4096,64]{1,0:T(8,128)(2,1)S(1)} reduce(bf16[4096,1,64]{2,1,0:T(2,128)(2,1)S(1)} %bitcast.60, bf16[]{:T(256)} %broadcast.96), dimensions={1}, to_apply=%bitcast.31.reduce_sub_computation | reduce | bytes 1048578
  37.9 6.0 %all-to-all-start.2 = ((bf16[8,2,16384]{2,1,0:T(2,128)(2,1)}), bf16[8,2,16384]{2,1,0:T(2,128)(2,1)}, u32[]{:S(2)}, u32[]{:S(2)}) async-start(bf16[8,2,16384]{2,1,0:T(2,128)(2,1)} %reshape.110), calls=%async_computation.2 | async-start | bytes 1048576 | tf_op jit(solution)/shard_map/all_to_all | solution.py:54
  43.9 3.2 %copy.39 = bf16[1,4096,128]{2,0,1:T(2,128)(2,1)S(1)} copy(bf16[1,4096,128]{2,1,0:T(8,128)(2,1)} %param.15) | data formatting | bytes 2097152 | tf_op args[1]
  47.1 22.3 %reduce = bf16[4096,128]{1,0:T(8,128)(2,1)S(1)} reduce(bf16[4096,1,128]{2,1,0:T(2,128)(2,1)S(1)} %bitcast.62, bf16[]{:T(256)} %broadcast.96), dimensions={1}, to_apply=%bitcast.45.reduce_sub_computation | reduce | bytes 2097154
  70.6 6.0 %all-to-all-start = ((bf16[8,2,32768]{2,1,0:T(2,128)(2,1)}), bf16[8,2,32768]{2,1,0:T(2,128)(2,1)}, u32[]{:S(2)}, u32[]{:S(2)}) async-start(bf16[8,2,32768]{2,1,0:T(2,128)(2,1)} %reshape.108), calls=%async_computation | async-start | bytes 2097152 | tf_op jit(solution)/shard_map/all_to_all | solution.py:55
  76.9 4.1 %reshape.111 = bf16[4096,1,64]{2,1,0:T(2,128)(2,1)S(1)} reshape(bf16[8,2,16384]{2,1,0:T(2,128)(2,1)} %all-to-all-done.2) | data formatting | bytes 1048576
  81.0 3.6 %copy.28 = bf16[1,4096,64]{1,2,0:T(8,128)(2,1)} copy(bf16[1,4096,64]{2,0,1:T(2,128)(2,1)S(1)} %bitcast.59) | data formatting | bytes 1048576 | tf_op jit(solution)/shard_map/all_to_all | solution.py:54
  84.7 16.9 %all-to-all-done = bf16[8,2,32768]{2,1,0:T(2,128)(2,1)} async-done(((bf16[8,2,32768]{2,1,0:T(2,128)(2,1)}), bf16[8,2,32768]{2,1,0:T(2,128)(2,1)}, u32[]{:S(2)}, u32[]{:S(2)}) %all-to-all-start) | async-done | bytes 1048608 | tf_op jit(solution)/shard_map/all_to_all | solution.py:55
  101.5 4.3 %reshape.109 = bf16[4096,1,128]{2,1,0:T(2,128)(2,1)S(1)} reshape(bf16[8,2,32768]{2,1,0:T(2,128)(2,1)} %all-to-all-done) | data formatting | bytes 2097152
  107.0 28.7 %while.29 = (s32[]{:T(128)}, f32[128,2048]{1,0:T(8,128)S(1)}, bf16[4096,128]{1,0:T(8,128)(2,1)}, bf16[4096,32]{0,1:T(8,128)(2,1)S(1)}, bf16[4096,64]{0,1:T(8,128...) while((s32[]{:T(128)}, f32[128,2048]{1,0:T(8,128)S(1)}, bf16[4096,128]{1,0:T(8,128)(2,1)}, ...), condition=%wide.region_1.2_spmd.clone, body=%wide.region_0.1_spmd.clone.sunk | while | flops 539492352 | bytes 11337897 | solution.py:81
  107.9 2.2 %broadcast_multiply_fusion.2 = bf16[1024,32,64]{0,2,1:T(8,128)(2,1)} fusion(bf16[1024,64]{0,1:T(8,128)(2,1)S(1)} %constant_dynamic-slice_fusion.4, bf16[1024,32]{0,1:T(8,128)(2,1)S(1)} %constant_dynamic-slice_fusion.5), kind=kLoop, calls=%fused_computation.3.clone.1 | loop fusion | flops 2097152 | bytes 4390912 | tf_op jit(solution)/shard_map/while/body/eval_jaxpr/mul | solution.py:75
  110.1 4.0 %convolution_add_fusion.2 = f32[128,2048]{1,0:T(8,128)S(1)} fusion(bf16[1024,2048]{0,1:T(8,128)(2,1)} %bitcast.56, f32[128,2048]{1,0:T(8,128)S(1)} %get-tuple-element.306, pred[]{:T(512)S(6)} %compare.16, bf16[4096,128]{1,0:T(8,128)(2,1)} %get-tuple-element.316, s32[]{:T(128)S(6)} %select_n.65), kind=kOutput, calls=%fused_computation.2.clone.1 | convolution fusion | flops 537395200 | bytes 6553605 | tf_op jit(solution)/shard_map/while/body/eval_jaxpr/dot_general | solution.py:76
  115.1 2.2 %broadcast_multiply_fusion.2 = bf16[1024,32,64]{0,2,1:T(8,128)(2,1)} fusion(bf16[1024,64]{0,1:T(8,128)(2,1)S(1)} %constant_dynamic-slice_fusion.4, bf16[1024,32]{0,1:T(8,128)(2,1)S(1)} %constant_dynamic-slice_fusion.5), kind=kLoop, calls=%fused_computation.3.clone.1 | loop fusion | flops 2097152 | bytes 4390912 | tf_op jit(solution)/shard_map/while/body/eval_jaxpr/mul | solution.py:75
  117.3 4.0 %convolution_add_fusion.2 = f32[128,2048]{1,0:T(8,128)S(1)} fusion(bf16[1024,2048]{0,1:T(8,128)(2,1)} %bitcast.56, f32[128,2048]{1,0:T(8,128)S(1)} %get-tuple-element.306, pred[]{:T(512)S(6)} %compare.16, bf16[4096,128]{1,0:T(8,128)(2,1)} %get-tuple-element.316, s32[]{:T(128)S(6)} %select_n.65), kind=kOutput, calls=%fused_computation.2.clone.1 | convolution fusion | flops 537395200 | bytes 6553605 | tf_op jit(solution)/shard_map/while/body/eval_jaxpr/dot_general | solution.py:76
  124.5 4.0 %convolution_add_fusion.2 = f32[128,2048]{1,0:T(8,128)S(1)} fusion(bf16[1024,2048]{0,1:T(8,128)(2,1)} %bitcast.56, f32[128,2048]{1,0:T(8,128)S(1)} %get-tuple-element.306, pred[]{:T(512)S(6)} %compare.16, bf16[4096,128]{1,0:T(8,128)(2,1)} %get-tuple-element.316, s32[]{:T(128)S(6)} %select_n.65), kind=kOutput, calls=%fused_computation.2.clone.1 | convolution fusion | flops 537395200 | bytes 6553605 | tf_op jit(solution)/shard_map/while/body/eval_jaxpr/dot_general | solution.py:76
  131.7 4.0 %convolution_add_fusion.2 = f32[128,2048]{1,0:T(8,128)S(1)} fusion(bf16[1024,2048]{0,1:T(8,128)(2,1)} %bitcast.56, f32[128,2048]{1,0:T(8,128)S(1)} %get-tuple-element.306, pred[]{:T(512)S(6)} %compare.16, bf16[4096,128]{1,0:T(8,128)(2,1)} %get-tuple-element.316, s32[]{:T(128)S(6)} %select_n.65), kind=kOutput, calls=%fused_computation.2.clone.1 | convolution fusion | flops 537395200 | bytes 6553605 | tf_op jit(solution)/shard_map/while/body/eval_jaxpr/dot_general | solution.py:76
  141.5 2.4 %copy.30 = bf16[32,128,64]{2,1,0:T(8,128)(2,1)} copy(bf16[32,128,64]{1,2,0:T(8,128)(2,1)} %fusion.3) | data formatting | bytes 1048576 | tf_op jit(solution)/shard_map/convert_element_type | solution.py:34
  143.9 2.7 %convert_element_type.24 = bf16[32,8192]{1,0:T(8,128)(2,1)} reshape(bf16[32,128,64]{2,1,0:T(8,128)(2,1)} %copy.30) | data formatting | bytes 1048576 | tf_op jit(solution)/shard_map/convert_element_type | solution.py:34
  146.6 32.4 %while.28 = (s32[]{:T(128)}, bf16[32,8192]{1,0:T(8,128)(2,1)}, bf16[128,192]{1,0:T(8,128)(2,1)S(1)}, bf16[192,8192]{1,0:T(8,128)(2,1)S(1)}, s32[3]{0:T(128)S(1)}...) while((s32[]{:T(128)}, bf16[32,8192]{1,0:T(8,128)(2,1)}, ...), condition=%wide.region_3.4_spmd, body=%wide.region_2.3_spmd.sunk | while | flops 100669456 | bytes 6832468 | solution.py:95
  151.8 5.6 %collective-permute-done = bf16[32,8192]{1,0:T(8,128)(2,1)} collective-permute-done((bf16[32,8192]{1,0:T(8,128)(2,1)}, bf16[32,8192]{1,0:T(8,128)(2,1)}, u32[]{:S(2)}, u32[]{:S(2)}) %collective-permute-start) | collective-permute-done | bytes 524320 | tf_op jit(solution)/shard_map/while/body/eval_jaxpr/ppermute | solution.py:14
  162.6 5.6 %collective-permute-done = bf16[32,8192]{1,0:T(8,128)(2,1)} collective-permute-done((bf16[32,8192]{1,0:T(8,128)(2,1)}, bf16[32,8192]{1,0:T(8,128)(2,1)}, u32[]{:S(2)}, u32[]{:S(2)}) %collective-permute-start) | collective-permute-done | bytes 524320 | tf_op jit(solution)/shard_map/while/body/eval_jaxpr/ppermute | solution.py:14
  173.4 5.6 %collective-permute-done = bf16[32,8192]{1,0:T(8,128)(2,1)} collective-permute-done((bf16[32,8192]{1,0:T(8,128)(2,1)}, bf16[32,8192]{1,0:T(8,128)(2,1)}, u32[]{:S(2)}, u32[]{:S(2)}) %collective-permute-start) | collective-permute-done | bytes 524320 | tf_op jit(solution)/shard_map/while/body/eval_jaxpr/ppermute | solution.py:14
  (55 shorter events, 38.1 us)
Async XLA Ops:
  0.0 135.7 %copy-start = (f32[128,128]{1,0:T(8,128)S(1)}, f32[128,128]{1,0:T(8,128)}, u32[]{:S(2)}) copy-start(f32[128,128]{1,0:T(8,128)} %param.22) | copy-start | bytes 196612
  1.4 36.5 %all-to-all-start.1 = ((s32[1,8,512]{2,0,1:T(1,128)}), s32[1,8,512]{2,0,1:T(1,128)S(1)}, u32[]{:S(2)}, u32[]{:S(2)}) async-start(s32[1,8,512]{2,0,1:T(1,128)} %bitcast.1), calls=%async_computation.1 | async-start | bytes 32768 | tf_op jit(solution)/shard_map/all_to_all | solution.py:56
  37.9 32.6 %all-to-all-start.2 = ((bf16[8,2,16384]{2,1,0:T(2,128)(2,1)}), bf16[8,2,16384]{2,1,0:T(2,128)(2,1)}, u32[]{:S(2)}, u32[]{:S(2)}) async-start(bf16[8,2,16384]{2,1,0:T(2,128)(2,1)} %reshape.110), calls=%async_computation.2 | async-start | bytes 1048576 | tf_op jit(solution)/shard_map/all_to_all | solution.py:54
  47.1 29.5 %copy-start.3 = (f32[64]{0:T(128)S(1)}, f32[64]{0:T(128)}, u32[]{:S(2)}) copy-start(f32[64]{0:T(128)} %param.19) | copy-start | bytes 772
  47.1 29.5 %copy-start.4 = (f32[128]{0:T(128)S(1)}, f32[128]{0:T(128)}, u32[]{:S(2)}) copy-start(f32[128]{0:T(128)} %param.20) | copy-start | bytes 1540
  47.1 29.6 %copy-start.5 = (s32[1,32]{1,0:T(1,128)S(1)}, s32[1,32]{1,0:T(1,128)}, u32[]{:S(2)}) copy-start(s32[1,32]{1,0:T(1,128)} %param.18) | copy-start | bytes 388
  70.6 31.0 %all-to-all-start = ((bf16[8,2,32768]{2,1,0:T(2,128)(2,1)}), bf16[8,2,32768]{2,1,0:T(2,128)(2,1)}, u32[]{:S(2)}, u32[]{:S(2)}) async-start(bf16[8,2,32768]{2,1,0:T(2,128)(2,1)} %reshape.108), calls=%async_computation | async-start | bytes 2097152 | tf_op jit(solution)/shard_map/all_to_all | solution.py:55
  107.0 30.5 %copy-start.2 = (f32[64,64]{1,0:T(8,128)S(1)}, f32[64,64]{1,0:T(8,128)}, u32[]{:S(2)}) copy-start(f32[64,64]{1,0:T(8,128)} %param.21) | copy-start | bytes 49156
  138.6 8.0 %copy-start.1 = (bf16[1,192,8192]{2,1,0:T(8,128)(2,1)S(1)}, bf16[1,192,8192]{2,1,0:T(8,128)(2,1)}, u32[]{:S(2)}) copy-start(bf16[1,192,8192]{2,1,0:T(8,128)(2,1)} %param.23) | copy-start | bytes 9437188
  148.5 8.9 %collective-permute-start = (bf16[32,8192]{1,0:T(8,128)(2,1)}, bf16[32,8192]{1,0:T(8,128)(2,1)}, u32[]{:S(2)}, u32[]{:S(2)}) collective-permute-start(bf16[32,8192]{1,0:T(8,128)(2,1)} %copy.51), channel_id=1, source_target_pairs={{0,1},{1,2},{2,3},{3,0},{4,5},{5,6},{6,7},{7,4},{8,9},{9,10},{10,1... | collective-permute-start | bytes 1572872 | tf_op jit(solution)/shard_map/while/body/eval_jaxpr/ppermute | solution.py:14
  159.3 8.9 %collective-permute-start = (bf16[32,8192]{1,0:T(8,128)(2,1)}, bf16[32,8192]{1,0:T(8,128)(2,1)}, u32[]{:S(2)}, u32[]{:S(2)}) collective-permute-start(bf16[32,8192]{1,0:T(8,128)(2,1)} %copy.51), channel_id=1, source_target_pairs={{0,1},{1,2},{2,3},{3,0},{4,5},{5,6},{6,7},{7,4},{8,9},{9,10},{10,1... | collective-permute-start | bytes 1572872 | tf_op jit(solution)/shard_map/while/body/eval_jaxpr/ppermute | solution.py:14
  170.1 8.9 %collective-permute-start = (bf16[32,8192]{1,0:T(8,128)(2,1)}, bf16[32,8192]{1,0:T(8,128)(2,1)}, u32[]{:S(2)}, u32[]{:S(2)}) collective-permute-start(bf16[32,8192]{1,0:T(8,128)(2,1)} %copy.51), channel_id=1, source_target_pairs={{0,1},{1,2},{2,3},{3,0},{4,5},{5,6},{6,7},{7,4},{8,9},{9,10},{10,1... | collective-permute-start | bytes 1572872 | tf_op jit(solution)/shard_map/while/body/eval_jaxpr/ppermute | solution.py:14
where the time goes:
time: 185 us; the launch traced here: 184 us
  other arithmetic  55.2 us (30%)
  local copies, waits for them, and re-layouts  43 us (23%)
  waiting for transfers between devices  33.7 us (18%)
  matrix products  30.1 us (16%)
  starting transfers between devices  19.3 us (10%)
  loops' own time  1.96 us (1%)
    unnamed x3, other arithmetic  44.6 us
    unnamed x20, local copies, waits for them, and re-layouts  20.8 us
    all_to_all x1, waiting for transfers between devices, on_device(): lax.all_to_all(out_rows, 'query', split_axis=1, concat_axis=1, tiled=True)  16.9 us
    ppermute x3, waiting for transfers between devices, from_behind(): lax.ppermute(x, axis, [(i, (i + by) % devices) for i in range(devices)])  16.9 us
    dot_general x4, matrix products, accumulate(): lax.dot_general(g_part, spread, (((0,), (0,)), ((), ())), preferred_eleme...  15.9 us
    mul x4, other arithmetic, accumulate(): w_part[:, :, None] * x_part[:, None, :]  8.93 us
    dot_general x4, matrix products, record(): lax.dot_general(query_block, train_slab, (((1,), (1,)), ((), ())), prefer...  8.42 us
    all_to_all x1, starting transfers between devices, on_device(): lax.all_to_all(packed_keys, 'query', split_axis=1, concat_axis=1, tiled=T...  7.31 us
  transfers between devices with their start and end apart: 6, of which 4 were waited for; matrix products, arithmetic and copies ran while one was open for 39% of the time, Pallas kernels for 0%

commit v1 on v0

v1 whole, which is shorter than its diff:
```python
import functools

import jax
import jax.numpy as jnp
from jax import lax
from jax.experimental import pallas as pl
from jax.experimental.pallas import tpu as pltpu
from jax.sharding import PartitionSpec as P

damping = 0.1
MESH = pl.DeviceIdType.MESH
f32 = jnp.float32
bf16 = jnp.bfloat16


def halves(x):
    high = x.astype(bf16)
    return high, (x - high.astype(f32)).astype(bf16)


def mm(a, b, ca, cb):
    return lax.dot_general(a, b, (((ca,), (cb,)), ((), ())), preferred_element_type=f32)


def kernel(
    queries, stores, x_ref, g_ref, key_ref, len_ref, eig_in_ref, eig_out_ref, bi_ref, bo_ref,
    train_ref, out_ref,
    x_got, g_got, key_got, train, acc, turn, feats,
    x_send, g_send, key_send, x_recv, g_recv, key_recv, own_sem, train_sem,
    far_send, far_recv, near_send, near_recv,
):
    me = lax.axis_index("query")
    column = lax.axis_index("store")
    chips = stores // 2
    chip, core = column // 2, column % 2
    partner = chip * 2 + (1 - core)
    cap = x_ref.shape[2]
    in_width, out_width = bi_ref.shape[0], bo_ref.shape[0]
    docs = len_ref.shape[1]
    half = docs // 2
    slab = train_ref.shape[0]

    train_copy = pltpu.make_async_copy(train_ref, train, train_sem)
    train_copy.start()

    def own_copies():
        rows = pl.ds(pl.multiple_of(me * cap, cap), cap)
        return (
            pltpu.make_async_copy(x_ref.at[me], x_got.at[0], own_sem.at[0]),
            pltpu.make_async_copy(g_ref.at[rows], g_got.at[0], own_sem.at[1]),
            pltpu.make_async_copy(key_ref.at[me], key_got.at[0], own_sem.at[2]),
        )

    for copy in own_copies():
        copy.start()

    barrier = pltpu.get_barrier_semaphore()

    def greet(m, carry):
        pl.semaphore_signal(
            barrier, inc=1, device_id={"query": (me + m) % queries}, device_id_type=MESH
        )
        return carry

    lax.fori_loop(1, queries, greet, 0)
    for d in range(1, chips):
        pl.semaphore_signal(
            barrier, inc=1, device_id={"store": (chip + d) % chips * 2 + core}, device_id_type=MESH
        )
    pl.semaphore_signal(barrier, inc=1, device_id={"store": partner}, device_id_type=MESH)
    pl.semaphore_wait(barrier, (queries - 1) + (chips - 1) + 1)

    def row_copies(m):
        target = (me + m) % queries
        rows = pl.ds(pl.multiple_of(target * cap, cap), cap)
        there = {"query": target}
        return (
            pltpu.make_async_remote_copy(
                key_ref.at[target], key_got.at[m], key_send.at[m], key_recv.at[m],
                device_id=there, device_id_type=MESH,
            ),
            pltpu.make_async_remote_copy(
                g_ref.at[rows], g_got.at[m], g_send.at[m], g_recv.at[m],
                device_id=there, device_id_type=MESH,
            ),
            pltpu.make_async_remote_copy(
                x_ref.at[target], x_got.at[m], x_send.at[m], x_recv.at[m],
                device_id=there, device_id_type=MESH,
            ),
        )

    middle = queries // 2

    def offset(n):
        return (middle + n) % queries

    def launch(n, carry):
        for copy in row_copies((middle + n) % queries):
            copy.start()
        return carry

    lax.fori_loop(0, middle, launch, 0)
    lax.fori_loop(middle + 1, queries, launch, 0)

    bo_high, bo_low = halves(bo_ref[...])
    first = jnp.concatenate([bo_high, bo_low], axis=1)
    first = jnp.concatenate([first, first], axis=0)
    last = jnp.concatenate(
        [
            jnp.concatenate([bo_high, bo_high], axis=1),
            jnp.concatenate([bo_low, bo_low], axis=1),
        ],
        axis=0,
    )
    bi_high, bi_low = halves(bi_ref[...])
    rotate = jnp.concatenate([bi_high, bi_high, bi_low, bi_low], axis=0)
    bt_high, bt_low = halves(bi_ref[...].T)
    restore = jnp.concatenate([bt_high, bt_high, bt_low, bt_low], axis=0)
    square = (in_width, in_width)
    diagonal = lax.broadcasted_iota(jnp.int32, square, 0) == lax.broadcasted_iota(
        jnp.int32, square, 1
    )
    eig_column = jnp.sum(
        jnp.where(diagonal, jnp.broadcast_to(eig_in_ref[...], square), 0.0), axis=1, keepdims=True
    )
    scaling = 1.0 / (eig_column * eig_out_ref[...] + damping)

    group = 8 * in_width

    def absorb(slot, fresh):
        keys = key_got[slot]
        doc = keys // 256
        place = keys % 256
        limit = jnp.zeros_like(doc)
        for e in range(docs):
            limit = jnp.where(doc == e, len_ref[0, e], limit)
        named = jnp.where(place < limit, doc, -1).astype(f32)
        named = jnp.broadcast_to(named, (16, cap)).astype(bf16)[None]
        inputs = x_got[slot].reshape(in_width // 16, 16, cap)
        grads = g_got[slot]
        for start in range(0, docs, 8):
            parts = []
            for c in range(start, start + 8):
                doc_here = (c % 2) * half + c // 2
                kept = jnp.where(
                    named == jnp.asarray(doc_here, bf16), inputs, jnp.zeros_like(inputs)
                )
                parts.append(kept.reshape(in_width, cap))
            spread = jnp.concatenate(parts, axis=0)
            rows = pl.ds(start * in_width, group)
            added = mm(spread, grads, 1, 0)
            if fresh:
                acc[rows, :] = added
            else:
                acc[rows, :] += added

    for copy in own_copies():
        copy.wait()
    absorb(0, True)

    def arrive(n, carry):
        m = (middle + n) % queries
        for copy in row_copies(m):
            copy.wait_recv()
        absorb(m, False)
        return carry

    lax.fori_loop(0, middle, arrive, 0)
    lax.fori_loop(middle + 1, queries, arrive, 0)

    for start in range(0, docs, 8):
        high, low = halves(acc[pl.ds(start * in_width, group), :])
        both = mm(jnp.concatenate([high, low], axis=1), first, 1, 0)
        rotated = both[:, :out_width] + both[:, out_width:]
        wide = jnp.concatenate(
            [rotated[c * in_width : (c + 1) * in_width] for c in range(8)], axis=1
        )
        high, low = halves(wide)
        turned = mm(rotate, jnp.concatenate([high, low, high, low], axis=0), 0, 0)
        turned = turned * jnp.concatenate([scaling] * 8, axis=1)
        high, low = halves(turned)
        restored = mm(restore, jnp.concatenate([high, low, high, low], axis=0), 0, 0)
        tall = jnp.concatenate(
            [restored[:, c * out_width : (c + 1) * out_width] for c in range(8)], axis=0
        )
        high, low = halves(tall)
        both = mm(last, jnp.concatenate([high, low], axis=1), 1, 1)
        final = both[:out_width] + both[out_width:]
        for a in range(4):
            turn[pl.ds(start // 2 + a, out_width, stride=half), :] = final[
                :, a * 2 * in_width : (a + 1) * 2 * in_width
            ]

    lane = lax.broadcasted_iota(jnp.int32, (half, 128), 1)

    def weave(p, carry):
        even = turn[pl.ds(pl.multiple_of(p * 2 * half, 8), half), :]
        odd = turn[pl.ds(pl.multiple_of(p * 2 * half + half, 8), half), :]
        columns = pl.ds(pl.multiple_of(p * 128, 128), 128)
        upper = jnp.where(lane < in_width, even, pltpu.roll(odd, in_width, 1))
        lower = jnp.where(lane < in_width, pltpu.roll(even, in_width, 1), odd)
        feats[0, pl.ds(0, half), columns] = upper.astype(bf16)
        feats[0, pl.ds(half, half), columns] = lower.astype(bf16)
        return carry

    lax.fori_loop(0, out_width // 2, weave, 0, unroll=8)

    def far_copy(d):
        return pltpu.make_async_remote_copy(
            feats.at[0], feats.at[2 * d], far_send.at[d], far_recv.at[d],
            device_id={"store": (chip + d) % chips * 2 + core}, device_id_type=MESH,
        )

    def near_copy(d):
        return pltpu.make_async_remote_copy(
            feats.at[2 * d], feats.at[2 * d + 1], near_send.at[d], near_recv.at[d],
            device_id={"store": partner}, device_id_type=MESH,
        )

    for d in range(1, chips):
        far_copy(d).start()
    near_copy(0).start()
    train_copy.wait()

    def score(slot, owner):
        result = mm(feats[slot], train[...], 1, 1)
        rows = pl.ds(pl.multiple_of(owner * docs, docs), docs)
        out_ref[rows, :] = result.astype(bf16)

    score(0, column)
    near_copy(0).wait_recv()
    score(1, partner)
    for d in range(1, chips):
        origin = (chip + chips - d) % chips * 2
        far_copy(d).wait_recv()
        near_copy(d).start()
        score(2 * d, origin + core)
        near_copy(d).wait_recv()
        score(2 * d + 1, origin + (1 - core))

    def drain(n, carry):
        for copy in row_copies((middle + n) % queries):
            copy.wait_send()
        return carry

    lax.fori_loop(0, middle, drain, 0)
    lax.fori_loop(middle + 1, queries, drain, 0)
    for d in range(1, chips):
        far_copy(d).wait_send()
    for d in range(chips):
        near_copy(d).wait_send()


def on_device(
    queries, stores,
    in_rows, out_rows, row_doc, row_pos, doc_len, eig_in, eig_out, basis_in, basis_out, train_feats,
):
    row_count, in_width = in_rows.shape[1:]
    out_width = out_rows.shape[2]
    docs = doc_len.shape[1]
    slab, feat = train_feats.shape[1:]
    cap = row_count // queries
    inputs = jnp.swapaxes(in_rows[0].reshape(queries, cap, in_width), 1, 2)
    keys = (row_doc * 256 + row_pos).reshape(queries, 1, cap)
    hbm = pl.BlockSpec(memory_space=pl.ANY)
    vmem = pl.BlockSpec(memory_space=pltpu.VMEM)
    smem = pl.BlockSpec(memory_space=pltpu.SMEM)
    dma = pltpu.SemaphoreType.DMA
    chips = stores // 2
    scores = pl.pallas_call(
        functools.partial(kernel, queries, stores),
        name="attribution",
        out_shape=jax.ShapeDtypeStruct((stores * docs, slab), bf16),
        in_specs=[hbm, hbm, hbm, smem, vmem, vmem, vmem, vmem, hbm],
        out_specs=vmem,
        scratch_shapes=[
            pltpu.VMEM((queries, in_width, cap), bf16),
            pltpu.VMEM((queries, cap, out_width), bf16),
            pltpu.VMEM((queries, 1, cap), jnp.int32),
            pltpu.VMEM((slab, feat), bf16),
            pltpu.VMEM((docs * in_width, out_width), f32),
            pltpu.VMEM((docs * in_width, out_width), f32),
            pltpu.VMEM((stores, docs, feat), bf16),
            dma((queries,)), dma((queries,)), dma((queries,)),
            dma((queries,)), dma((queries,)), dma((queries,)),
            dma((3,)), dma,
            dma((chips,)), dma((chips,)), dma((chips,)), dma((chips,)),
        ],
        compiler_params=pltpu.CompilerParams(
            collective_id=0, has_side_effects=True, vmem_limit_bytes=48 * 1024 * 1024
        ),
    )(
        inputs, out_rows[0], keys, doc_len, eig_in[None], eig_out[None], basis_in, basis_out,
        train_feats[0],
    )
    return scores[None]


def solution(mesh):
    placed = (
        P("query", "store", None),
        P("query", "store", None),
        P("query", "store"),
        P("query", "store"),
        P("query", "store"),
        P(),
        P(),
        P(),
        P(),
        P("query", "store", None),
    )
    return jax.shard_map(
        functools.partial(on_device, mesh.shape["query"], mesh.shape["store"]),
        mesh=mesh, in_specs=placed, out_specs=P("query", None, "store"), check_vma=False,
    )
```

time: 185 us -> 73.9 us (0.40)
  the two profiles are of different devices: /device:TPU:0 before, /device:TPU:13 now
where the time goes in v1:
time: 73.9 us; the launch traced here: 73.5 us
  Pallas kernels  63.9 us (86%)
  local copies, waits for them, and re-layouts  8.76 us (12%)
  other arithmetic  0.76 us (1%)
    pallas_call x1, Pallas kernels, on_device(): pl.pallas_call(functools.partial(kernel, queries, stores), name='attribut...  63.9 us
    unnamed x15, local copies, waits for them, and re-layouts  7.88 us

profile of v1, /device:TPU:13, one launch (start us, length us, event | category | flops | bytes accessed | tf_op | source)
XLA Modules:
  0.0 73.5 jit_solution(6132228907020423353)
XLA Ops:
  0.0 1.2 %copy.14 = bf16[8,8,8,512]{3,2,1,0:T(8,128)(2,1)S(1)} copy(bf16[8,8,8,512]{3,1,2,0:T(8,128)(2,1)} %bitcast.22) | data formatting | bytes 1048576
  1.2 0.2 copy.16
  1.4 0.8 %multiply_add_fusion = s32[1,4096]{1,0:T(1,128)S(1)} fusion(s32[1,4096]{1,0:T(1,128)} %param.13, s32[1,4096]{1,0:T(1,128)} %param.12), kind=kLoop, calls=%fused_computation.1 | loop fusion | flops 8192 | bytes 49152 | tf_op jit(solution)/shard_map/add | solution.py:264
  2.1 0.0 copy-start
  2.2 1.9 %copy-done = bf16[1,192,8192]{2,1,0:T(8,128)(2,1)S(1)} copy-done((bf16[1,192,8192]{2,1,0:T(8,128)(2,1)S(1)}, bf16[1,192,8192]{2,1,0:T(8,128)(2,1)}, u32[]{:S(2)}) %copy-start) | copy-done | bytes 3145752
  4.0 0.0 copy-start.1
  4.0 1.2 %copy-done.1 = bf16[1,4096,128]{2,1,0:T(8,128)(2,1)S(1)} copy-done((bf16[1,4096,128]{2,1,0:T(8,128)(2,1)S(1)}, bf16[1,4096,128]{2,1,0:T(8,128)(2,1)}, u32[]{:S(2)}) %copy-start.1) | copy-done | bytes 1048600
  5.3 0.0 copy-start.2
  5.3 0.8 %copy-done.2 = f32[128,128]{1,0:T(8,128)S(1)} copy-done((f32[128,128]{1,0:T(8,128)S(1)}, f32[128,128]{1,0:T(8,128)}, u32[]{:S(2)}) %copy-start.2) | copy-done | bytes 65560
  6.1 0.0 copy-start.3
  6.1 0.8 %copy-done.3 = f32[64,64]{1,0:T(8,128)S(1)} copy-done((f32[64,64]{1,0:T(8,128)S(1)}, f32[64,64]{1,0:T(8,128)}, u32[]{:S(2)}) %copy-start.3) | copy-done | bytes 16408
  6.9 0.0 copy-start.4
  6.9 0.7 copy-done.4
  7.5 0.0 copy-start.5
  7.5 0.7 copy-done.5
  8.2 0.0 copy-start.6
  8.2 0.7 copy-done.6
  8.8 63.9 %attribution.1 = bf16[128,192]{1,0:T(8,128)(2,1)S(1)} custom-call(bf16[8,64,512]{2,1,0:T(8,128)(2,1)S(1)} %bitcast.15, bf16[4096,128]{1,0:T(8,128)(2,1)S(1)} %bitcast.16, s32[8,1,512]{2,1,0:T(1,128)S(1)} %bitcast.18, s32[1,32]{1,0:T(1,128)S(1)} %copy-done.4, f32[1,64]{1,0:T(1,128)S(1)} %bitcast.19, f32[1,128]{1,0:T(1,128)S(1)} %bitcast.20, ...), custom_call_target="tpu_custom_call" | custom-call | tf_op jit(solution)/shard_map/attribution/pallas_call | solution.py:270
  72.7 0.7 copy.13
Async XLA Ops:
  2.1 1.9 %copy-start = (bf16[1,192,8192]{2,1,0:T(8,128)(2,1)S(1)}, bf16[1,192,8192]{2,1,0:T(8,128)(2,1)}, u32[]{:S(2)}) copy-start(bf16[1,192,8192]{2,1,0:T(8,128)(2,1)} %param.19) | copy-start | bytes 9437188
  4.0 1.2 %copy-start.1 = (bf16[1,4096,128]{2,1,0:T(8,128)(2,1)S(1)}, bf16[1,4096,128]{2,1,0:T(8,128)(2,1)}, u32[]{:S(2)}) copy-start(bf16[1,4096,128]{2,1,0:T(8,128)(2,1)} %param.11) | copy-start | bytes 3145732
  5.3 0.8 %copy-start.2 = (f32[128,128]{1,0:T(8,128)S(1)}, f32[128,128]{1,0:T(8,128)}, u32[]{:S(2)}) copy-start(f32[128,128]{1,0:T(8,128)} %bo_ref.1) | copy-start | bytes 196612
  6.1 0.8 %copy-start.3 = (f32[64,64]{1,0:T(8,128)S(1)}, f32[64,64]{1,0:T(8,128)}, u32[]{:S(2)}) copy-start(f32[64,64]{1,0:T(8,128)} %bi_ref.1) | copy-start | bytes 49156
  6.9 0.7 copy-start.4
  7.5 0.7 copy-start.5
  8.2 0.7 copy-start.6

commit v2 on v1

--- a/solution.py
+++ b/solution.py
@@ -23,10 +23,11 @@
 
 
 def kernel(
-    queries, stores, x_ref, g_ref, key_ref, len_ref, eig_in_ref, eig_out_ref, bi_ref, bo_ref,
+    queries, stores, x_ref, g_ref, doc_ref, pos_ref, len_hbm, eig_in_hbm, eig_out_hbm, bi_hbm, bo_hbm,
     train_ref, out_ref,
-    x_got, g_got, key_got, train, acc, turn, feats,
-    x_send, g_send, key_send, x_recv, g_recv, key_recv, own_sem, train_sem,
+    len_ref, eig_in_ref, eig_out_ref, bi_ref, bo_ref, small_sem,
+    x_got, g_got, doc_got, pos_got, train, acc, turn, feats,
+    x_send, g_send, doc_send, pos_send, x_recv, g_recv, doc_recv, pos_recv, own_sem, train_sem,
     far_send, far_recv, near_send, near_recv,
 ):
     me = lax.axis_index("query")
@@ -34,25 +35,33 @@
     chips = stores // 2
     chip, core = column // 2, column % 2
     partner = chip * 2 + (1 - core)
-    cap = x_ref.shape[2]
+    cap = g_ref.shape[0] // queries
     in_width, out_width = bi_ref.shape[0], bo_ref.shape[0]
     docs = len_ref.shape[1]
     half = docs // 2
     slab = train_ref.shape[0]
 
+    small_copies = [
+        pltpu.make_async_copy(there, here, small_sem.at[n])
+        for n, (there, here) in enumerate(
+            (
+                (len_hbm, len_ref),
+                (eig_in_hbm, eig_in_ref),
+                (eig_out_hbm, eig_out_ref),
+                (bi_hbm, bi_ref),
+                (bo_hbm, bo_ref),
+            )
+        )
+    ]
     train_copy = pltpu.make_async_copy(train_ref, train, train_sem)
-    train_copy.start()
-
     def own_copies():
         rows = pl.ds(pl.multiple_of(me * cap, cap), cap)
         return (
-            pltpu.make_async_copy(x_ref.at[me], x_got.at[0], own_sem.at[0]),
+            pltpu.make_async_copy(x_ref.at[:, rows], x_got.at[0], own_sem.at[0]),
             pltpu.make_async_copy(g_ref.at[rows], g_got.at[0], own_sem.at[1]),
-            pltpu.make_async_copy(key_ref.at[me], key_got.at[0], own_sem.at[2]),
-        )
-
-    for copy in own_copies():
-        copy.start()
+            pltpu.make_async_copy(doc_ref.at[:, rows], doc_got.at[0], own_sem.at[2]),
+            pltpu.make_async_copy(pos_ref.at[:, rows], pos_got.at[0], own_sem.at[3]),
+        )
 
     barrier = pltpu.get_barrier_semaphore()
 
@@ -76,7 +85,11 @@
         there = {"query": target}
         return (
             pltpu.make_async_remote_copy(
-                key_ref.at[target], key_got.at[m], key_send.at[m], key_recv.at[m],
+                doc_ref.at[:, rows], doc_got.at[m], doc_send.at[m], doc_recv.at[m],
+                device_id=there, device_id_type=MESH,
+            ),
+            pltpu.make_async_remote_copy(
+                pos_ref.at[:, rows], pos_got.at[m], pos_send.at[m], pos_recv.at[m],
                 device_id=there, device_id_type=MESH,
             ),
             pltpu.make_async_remote_copy(
@@ -84,15 +97,12 @@
                 device_id=there, device_id_type=MESH,
             ),
             pltpu.make_async_remote_copy(
-                x_ref.at[target], x_got.at[m], x_send.at[m], x_recv.at[m],
+                x_ref.at[:, rows], x_got.at[m], x_send.at[m], x_recv.at[m],
                 device_id=there, device_id_type=MESH,
             ),
         )
 
     middle = queries // 2
-
-    def offset(n):
-        return (middle + n) % queries
 
     def launch(n, carry):
         for copy in row_copies((middle + n) % queries):
@@ -101,6 +111,13 @@
 
     lax.fori_loop(0, middle, launch, 0)
     lax.fori_loop(middle + 1, queries, launch, 0)
+    for copy in small_copies:
+        copy.start()
+    for copy in own_copies():
+        copy.start()
+    train_copy.start()
+    for copy in small_copies:
+        copy.wait()
 
     bo_high, bo_low = halves(bo_ref[...])
     first = jnp.concatenate([bo_high, bo_low], axis=1)
@@ -128,9 +145,8 @@
     group = 8 * in_width
 
     def absorb(slot, fresh):
-        keys = key_got[slot]
-        doc = keys // 256
-        place = keys % 256
+        doc = doc_got[slot]
+        place = pos_got[slot]
         limit = jnp.zeros_like(doc)
         for e in range(docs):
             limit = jnp.where(doc == e, len_ref[0, e], limit)
@@ -260,37 +276,41 @@
     docs = doc_len.shape[1]
     slab, feat = train_feats.shape[1:]
     cap = row_count // queries
-    inputs = jnp.swapaxes(in_rows[0].reshape(queries, cap, in_width), 1, 2)
-    keys = (row_doc * 256 + row_pos).reshape(queries, 1, cap)
-    hbm = pl.BlockSpec(memory_space=pl.ANY)
+    hbm = pl.BlockSpec(memory_space=pltpu.HBM)
     vmem = pl.BlockSpec(memory_space=pltpu.VMEM)
-    smem = pl.BlockSpec(memory_space=pltpu.SMEM)
     dma = pltpu.SemaphoreType.DMA
     chips = stores // 2
     scores = pl.pallas_call(
         functools.partial(kernel, queries, stores),
         name="attribution",
         out_shape=jax.ShapeDtypeStruct((stores * docs, slab), bf16),
-        in_specs=[hbm, hbm, hbm, smem, vmem, vmem, vmem, vmem, hbm],
+        in_specs=[hbm] * 10,
         out_specs=vmem,
         scratch_shapes=[
+            pltpu.SMEM((1, docs), jnp.int32),
+            pltpu.VMEM((1, in_width), f32),
+            pltpu.VMEM((1, out_width), f32),
+            pltpu.VMEM((in_width, in_width), f32),
+            pltpu.VMEM((out_width, out_width), f32),
+            dma((5,)),
             pltpu.VMEM((queries, in_width, cap), bf16),
             pltpu.VMEM((queries, cap, out_width), bf16),
+            pltpu.VMEM((queries, 1, cap), jnp.int32),
             pltpu.VMEM((queries, 1, cap), jnp.int32),
             pltpu.VMEM((slab, feat), bf16),
             pltpu.VMEM((docs * in_width, out_width), f32),
             pltpu.VMEM((docs * in_width, out_width), f32),
             pltpu.VMEM((stores, docs, feat), bf16),
-            dma((queries,)), dma((queries,)), dma((queries,)),
-            dma((queries,)), dma((queries,)), dma((queries,)),
-            dma((3,)), dma,
+            dma((queries,)), dma((queries,)), dma((queries,)), dma((queries,)),
+            dma((queries,)), dma((queries,)), dma((queries,)), dma((queries,)),
+            dma((4,)), dma,
             dma((chips,)), dma((chips,)), dma((chips,)), dma((chips,)),
         ],
         compiler_params=pltpu.CompilerParams(
-            collective_id=0, has_side_effects=True, vmem_limit_bytes=48 * 1024 * 1024
+            collective_id=0, has_side_effects=True, vmem_limit_bytes=67043328
         ),
     )(
-        inputs, out_rows[0], keys, doc_len, eig_in[None], eig_out[None], basis_in, basis_out,
+        in_rows[0].T, out_rows[0], row_doc, row_pos, doc_len, eig_in[None], eig_out[None], basis_in, basis_out,
         train_feats[0],
     )
     return scores[None]

time: 73.9 us -> 66 us (0.89)
  local copies, waits for them, and re-layouts: 8.76 us -> 1.56 us
  other arithmetic: 0.76 us -> 0 us
    unnamed x15 -> x0, local copies, waits for them, and re-layouts: 7.88 us -> none
    broadcast_in_dim x1, local copies, waits for them, and re-layouts: 0.72 us -> 1.56 us  [on_device(): return scores[None]]
    add x1 -> x0, other arithmetic: 0.76 us -> none  [on_device(): keys = (row_doc * 256 + row_pos).reshape(queries, 1, cap)]
where the time goes in v2:
time: 66 us; the launch traced here: 65.8 us
  Pallas kernels  64.2 us (97%)
  local copies, waits for them, and re-layouts  1.56 us (2%)
    pallas_call x1, Pallas kernels, on_device(): pl.pallas_call(functools.partial(kernel, queries, stores), name='attribut...  64.2 us
    broadcast_in_dim x1, local copies, waits for them, and re-layouts, on_device(): return scores[None]  1.56 us

profile of v2, /device:TPU:13, one launch (start us, length us, event | category | flops | bytes accessed | tf_op | source)
XLA Modules:
  0.0 65.8 jit_solution(10764526106333155794)
XLA Ops:
  0.0 64.2 %attribution.1 = bf16[128,192]{1,0:T(8,128)(2,1)} custom-call(bf16[64,4096]{1,0:T(8,128)(2,1)} %bitcast.10, bf16[4096,128]{1,0:T(8,128)(2,1)} %bitcast.9, s32[1,4096]{1,0:T(1,128)} %doc_ref.1, s32[1,4096]{1,0:T(1,128)} %pos_ref.1, s32[1,32]{1,0:T(1,128)} %len_hbm.1, f32[1,64]{1,0:T(1,128)} %bitcast.12, f32[1,128]{1,0:T(1,128)} %bitcast.13, f32[64,64]{1,0:T(8,128)} %bi_hbm.1, ...), custom_call_target="tpu_custom_call" | custom-call | tf_op jit(solution)/shard_map/attribution/pallas_call | solution.py:283
  64.2 1.6 %copy.11 = bf16[1,128,192]{1,2,0:T(8,128)(2,1)} copy(bf16[1,128,192]{2,1,0:T(8,128)(2,1)} %bitcast.11) | data formatting | bytes 98304 | tf_op jit(solution)/shard_map/broadcast_in_dim | solution.py:316

commit v3 on v2

--- a/solution.py
+++ b/solution.py
@@ -38,8 +38,11 @@
     cap = g_ref.shape[0] // queries
     in_width, out_width = bi_ref.shape[0], bo_ref.shape[0]
     docs = len_ref.shape[1]
-    half = docs // 2
-    slab = train_ref.shape[0]
+    batch = 16
+    batches = docs // batch
+    half = batch // 2
+    spans = 2
+    span = train_ref.shape[1] // spans
 
     small_copies = [
         pltpu.make_async_copy(there, here, small_sem.at[n])
@@ -157,7 +160,7 @@
         for start in range(0, docs, 8):
             parts = []
             for c in range(start, start + 8):
-                doc_here = (c % 2) * half + c // 2
+                doc_here = c // batch * batch + (c % 2) * half + c % batch // 2
                 kept = jnp.where(
                     named == jnp.asarray(doc_here, bf16), inputs, jnp.zeros_like(inputs)
                 )
@@ -184,7 +187,31 @@
     lax.fori_loop(0, middle, arrive, 0)
     lax.fori_loop(middle + 1, queries, arrive, 0)
 
-    for start in range(0, docs, 8):
+    def far_copy(d, k, h):
+        rows, columns = pl.ds(k * batch, batch), pl.ds(h * span, span)
+        return pltpu.make_async_remote_copy(
+            feats.at[0, rows, columns], feats.at[2 * d, rows, columns],
+            far_send.at[d, k, h], far_recv.at[d, k, h],
+            device_id={"store": (chip + d) % chips * 2 + core}, device_id_type=MESH,
+        )
+
+    def near_copy(d, k, h):
+        rows, columns = pl.ds(k * batch, batch), pl.ds(h * span, span)
+        return pltpu.make_async_remote_copy(
+            feats.at[2 * d, rows, columns], feats.at[2 * d + 1, rows, columns],
+            near_send.at[d, k, h], near_recv.at[d, k, h],
+            device_id={"store": partner}, device_id_type=MESH,
+        )
+
+    pieces = [(k, h) for k in range(batches) for h in range(spans)]
+    lane = lax.broadcasted_iota(jnp.int32, (half, 128), 1)
+
+    def depart(piece):
+        for d in range(1, chips):
+            far_copy(d, *piece).start()
+        near_copy(0, *piece).start()
+
+    def condition(start):
         high, low = halves(acc[pl.ds(start * in_width, group), :])
         both = mm(jnp.concatenate([high, low], axis=1), first, 1, 0)
         rotated = both[:, :out_width] + both[:, out_width:]
@@ -202,57 +229,68 @@
         high, low = halves(tall)
         both = mm(last, jnp.concatenate([high, low], axis=1), 1, 1)
         final = both[:out_width] + both[out_width:]
+        k, inside = start // batch, start % batch
         for a in range(4):
-            turn[pl.ds(start // 2 + a, out_width, stride=half), :] = final[
+            turn[k, pl.ds(inside // 2 + a, out_width, stride=half), :] = final[
                 :, a * 2 * in_width : (a + 1) * 2 * in_width
             ]
 
-    lane = lax.broadcasted_iota(jnp.int32, (half, 128), 1)
-
-    def weave(p, carry):
-        even = turn[pl.ds(pl.multiple_of(p * 2 * half, 8), half), :]
-        odd = turn[pl.ds(pl.multiple_of(p * 2 * half + half, 8), half), :]
-        columns = pl.ds(pl.multiple_of(p * 128, 128), 128)
-        upper = jnp.where(lane < in_width, even, pltpu.roll(odd, in_width, 1))
-        lower = jnp.where(lane < in_width, pltpu.roll(even, in_width, 1), odd)
-        feats[0, pl.ds(0, half), columns] = upper.astype(bf16)
-        feats[0, pl.ds(half, half), columns] = lower.astype(bf16)
-        return carry
-
-    lax.fori_loop(0, out_width // 2, weave, 0, unroll=8)
-
-    def far_copy(d):
-        return pltpu.make_async_remote_copy(
-            feats.at[0], feats.at[2 * d], far_send.at[d], far_recv.at[d],
-            device_id={"store": (chip + d) % chips * 2 + core}, device_id_type=MESH,
-        )
-
-    def near_copy(d):
-        return pltpu.make_async_remote_copy(
-            feats.at[2 * d], feats.at[2 * d + 1], near_send.at[d], near_recv.at[d],
-            device_id={"store": partner}, device_id_type=MESH,
-        )
-
-    for d in range(1, chips):
-        far_copy(d).start()
-    near_copy(0).start()
+    for n, (k, h) in enumerate(pieces):
+        if h == 0:
+            for start in range(k * batch, (k + 1) * batch, 8):
+                condition(start)
+
+        def weave(p, carry, k=k):
+            even = turn[k, pl.ds(pl.multiple_of(p * 2 * half, 8), half), :]
+            odd = turn[k, pl.ds(pl.multiple_of(p * 2 * half + half, 8), half), :]
+            columns = pl.ds(pl.multiple_of(p * 128, 128), 128)
+            upper = jnp.where(lane < in_width, even, pltpu.roll(odd, in_width, 1))
+            lower = jnp.where(lane < in_width, pltpu.roll(even, in_width, 1), odd)
+            feats[0, pl.ds(k * batch, batch), columns] = jnp.concatenate(
+                [upper, lower], axis=0
+            ).astype(bf16)
+            return carry
+
+        tiles = span // 128
+        lax.fori_loop(h * tiles, (h + 1) * tiles, weave, 0, unroll=8)
+        if n > 0:
+            depart(pieces[n - 1])
     train_copy.wait()
-
-    def score(slot, owner):
-        result = mm(feats[slot], train[...], 1, 1)
-        rows = pl.ds(pl.multiple_of(owner * docs, docs), docs)
-        out_ref[rows, :] = result.astype(bf16)
-
-    score(0, column)
-    near_copy(0).wait_recv()
-    score(1, partner)
-    for d in range(1, chips):
+    depart(pieces[-1])
+
+    def put(owner, k, rows, values):
+        start = pl.multiple_of(owner * docs + k * batch, batch)
+        out_ref[pl.ds(start, rows), :] = values.astype(bf16)
+
+    put(column, 0, docs, mm(feats[0], train[...], 1, 1))
+    for piece in pieces:
+        near_copy(0, *piece).wait_recv()
+    put(partner, 0, docs, mm(feats[1], train[...], 1, 1))
+
+    steps = [(d, k, h) for d in range(1, chips) for k, h in pieces]
+    totals = []
+
+    def finish(step):
+        d, k, h = step
+        near_copy(d, k, h).wait_recv()
+        columns = pl.ds(h * span, span)
+        queried = feats[2 * d : 2 * d + 2, pl.ds(k * batch, batch), columns]
+        part = mm(queried.reshape(2 * batch, span), train[:, columns], 1, 1)
+        total = part if h == 0 else totals.pop() + part
+        if h < spans - 1:
+            totals.append(total)
+            return
         origin = (chip + chips - d) % chips * 2
-        far_copy(d).wait_recv()
-        near_copy(d).start()
-        score(2 * d, origin + core)
-        near_copy(d).wait_recv()
-        score(2 * d + 1, origin + (1 - core))
+        put(origin + core, k, batch, total[:batch])
+        put(origin + (1 - core), k, batch, total[batch:])
+
+    for n, step in enumerate(steps):
+        far_copy(*step).wait_recv()
+        near_copy(*step).start()
+        if n > 0:
+            finish(steps[n - 1])
+    if steps:
+        finish(steps[-1])
 
     def drain(n, carry):
         for copy in row_copies((middle + n) % queries):
@@ -261,10 +299,11 @@
 
     lax.fori_loop(0, middle, drain, 0)
     lax.fori_loop(middle + 1, queries, drain, 0)
-    for d in range(1, chips):
-        far_copy(d).wait_send()
-    for d in range(chips):
-        near_copy(d).wait_send()
+    for piece in pieces:
+        for d in range(1, chips):
+            far_copy(d, *piece).wait_send()
+        for d in range(chips):
+            near_copy(d, *piece).wait_send()
 
 
 def on_device(
@@ -299,12 +338,12 @@
             pltpu.VMEM((queries, 1, cap), jnp.int32),
             pltpu.VMEM((slab, feat), bf16),
             pltpu.VMEM((docs * in_width, out_width), f32),
-            pltpu.VMEM((docs * in_width, out_width), f32),
+            pltpu.VMEM((docs // 16, 8 * out_width, 128), f32),
             pltpu.VMEM((stores, docs, feat), bf16),
             dma((queries,)), dma((queries,)), dma((queries,)), dma((queries,)),
             dma((queries,)), dma((queries,)), dma((queries,)), dma((queries,)),
             dma((4,)), dma,
-            dma((chips,)), dma((chips,)), dma((chips,)), dma((chips,)),
+            *[dma((chips, docs // 16, 2))] * 4,
         ],
         compiler_params=pltpu.CompilerParams(
             collective_id=0, has_side_effects=True, vmem_limit_bytes=67043328

time: 66 us -> 64.3 us (0.974)
  Pallas kernels: 64.2 us -> 62.6 us
    pallas_call x1, Pallas kernels: 64.2 us -> 62.6 us  [on_device(): pl.pallas_call(functools.partial(kernel, queries, stores), name='attribut...]
where the time goes in v3:
time: 64.3 us; the launch traced here: 64.1 us
  Pallas kernels  62.6 us (97%)
  local copies, waits for them, and re-layouts  1.56 us (2%)
    pallas_call x1, Pallas kernels, on_device(): pl.pallas_call(functools.partial(kernel, queries, stores), name='attribut...  62.6 us
    broadcast_in_dim x1, local copies, waits for them, and re-layouts, on_device(): return scores[None]  1.56 us

profile of v3, /device:TPU:13, one launch (start us, length us, event | category | flops | bytes accessed | tf_op | source)
XLA Modules:
  0.0 64.1 jit_solution(15629588316292416480)
XLA Ops:
  0.0 62.6 %attribution.1 = bf16[128,192]{1,0:T(8,128)(2,1)} custom-call(bf16[64,4096]{1,0:T(8,128)(2,1)} %bitcast.10, bf16[4096,128]{1,0:T(8,128)(2,1)} %bitcast.9, s32[1,4096]{1,0:T(1,128)} %doc_ref.1, s32[1,4096]{1,0:T(1,128)} %pos_ref.1, s32[1,32]{1,0:T(1,128)} %len_hbm.1, f32[1,64]{1,0:T(1,128)} %bitcast.12, f32[1,128]{1,0:T(1,128)} %bitcast.13, f32[64,64]{1,0:T(8,128)} %bi_hbm.1, ...), custom_call_target="tpu_custom_call" | custom-call | tf_op jit(solution)/shard_map/attribution/pallas_call | solution.py:322
  62.6 1.6 %copy.11 = bf16[1,128,192]{1,2,0:T(8,128)(2,1)} copy(bf16[1,128,192]{2,1,0:T(8,128)(2,1)} %bitcast.11) | data formatting | bytes 98304 | tf_op jit(solution)/shard_map/broadcast_in_dim | solution.py:355
